TPU v7x, 512 devices: a whole 4x4x16 slice. The times are simulated.
512 devices in a mesh: expert: 128 (over x, z_lo, y), dp: 4 (over z_hi, core).
Axes of the slice: x: 4, y: 4, z: 16 (z_hi: 2, z_lo: 8; z = z_hi * 8 + z_lo), core: 2. Of those that a mesh axis runs over, the one named last changes fastest.
Arguments:
- tokens: bfloat16 [8192, 2048], P(('expert', 'dp')), may hold values from -6 to 6
- cotangent: bfloat16 [8192, 2048], P(('expert', 'dp')), may hold values from -6 to 6
- route_ids: int32 [8192, 8], P(('expert', 'dp')), may hold values from 0 to 127, all different within a row; in each aligned block of 16 rows (0 to 15, 16 to 31, ...) at most 2 rows name the same one
- route_gates: bfloat16 [8192, 8], P(('expert', 'dp')), may hold values from 0.019897461 to 0.5
- gate_up: bfloat16 [128, 2048, 1536], P('expert', 'dp'), may hold values from -0.125 to 0.125
- down: bfloat16 [128, 2048, 768], P('expert', 'dp'), may hold values from -6 to 6
- moment1: bfloat16 [128, 2048, 768], P('expert', 'dp'), may hold values from -4 to 4
- moment2: bfloat16 [128, 2048, 768], P('expert', 'dp'), may hold values from 0.049804688 to 0.5
- placement: int32 [128], replicated, may hold values from 0 to 127, each once
Outputs:
- rollout_down: bfloat16 [128, 2048, 768], P('expert', None, 'dp')
Inputs may be any that keep to these rules, and one draw needn't show every extreme that they name: `route_ids`: each row names 8 different experts; within the rows of one device no expert is named more than 2 times, a bound that some block reaches. `placement`: each expert exactly once.
All inputs are finite; a program needn't handle non-finite values.
Results may differ from a plain program's by a relative error of at most 0.003.
Values may be sent and summed in bfloat16 or wider, within the bound.
A program may use at most 64 MiB of HBM per device.

v0:
```python
import jax
import jax.numpy as jnp
from jax import lax
from jax.sharding import Mesh, PartitionSpec as P

OPT_STEP = 2
BETA_ONE = 0.9
BETA_TWO = 0.95
ADAM_EPS = 1e-08
LEARN_RATE = 0.25
DP = ("zh", "core")
PLANE = ("x", "y")
EXPERT = ("x", "zl", "y")
CAP = 2
META = 128
contract_rows = (((0,), (0,)), ((), ()))


def pickers(meta, blocks, block_rows, top):
    plane = lax.axis_size(PLANE)
    wide = meta.shape[0]
    ids = meta[:, :top].astype(jnp.int32)
    gates = meta[:, top : 2 * top].astype(jnp.float32)
    place = jnp.arange(plane, dtype=jnp.int32)
    y_size = lax.axis_size("y")
    wanted = (
        place // y_size * lax.axis_size("zl") + lax.axis_index("zl")
    ) * y_size + place % y_size
    match = (ids[:, :, None] == wanted).astype(jnp.float32)
    hits = jnp.sum(match, axis=1)
    worth = jnp.sum(match * gates[:, :, None], axis=1)
    token = jnp.arange(wide, dtype=jnp.int32)
    own_block = token // block_rows
    before = (
        (own_block[:, None] == own_block[None, :]) & (token[None, :] < token[:, None])
    ).astype(jnp.bfloat16)
    earlier = jnp.dot(before, hits.astype(jnp.bfloat16), preferred_element_type=jnp.float32)
    row = jnp.arange(plane * blocks * CAP, dtype=jnp.int32)
    row_place = row // (blocks * CAP)
    spread = (row_place[:, None] == place[None, :]).astype(jnp.bfloat16)
    take = lambda v: lax.dot_general(
        spread, v.astype(jnp.bfloat16), (((1,), (1,)), ((), ())), preferred_element_type=jnp.float32
    )
    here = (row // CAP % blocks)[:, None] == own_block[None, :]
    slot = jnp.where(hits > 0, earlier, -1.0)
    chosen = here & (take(slot) == (row % CAP)[:, None].astype(jnp.float32))
    one_hot = chosen.astype(jnp.bfloat16)
    return (one_hot, jnp.where(chosen, take(worth), 0.0).astype(jnp.bfloat16))


def shards(tokens, cotangent, route_ids, route_gates, gate_up, down, moment1, moment2, placement):
    tok_rows, width = tokens.shape
    top = route_ids.shape[1]
    hidden_units = down.shape[2]
    groups = lax.axis_size(DP)
    line = lax.axis_size("zl")
    plane = lax.axis_size(PLANE)
    experts = lax.axis_size(EXPERT)
    share = width // groups
    bf16 = jnp.bfloat16
    meta = jnp.concatenate(
        [route_ids.astype(bf16), route_gates, jnp.zeros((tok_rows, META - 2 * top), bf16)], axis=1
    )
    tok_pack = lax.all_gather(jnp.concatenate([tokens, meta], axis=1), "zl", axis=0, tiled=True)
    cot_parts = cotangent.reshape(tok_rows, groups, share).transpose(1, 0, 2)
    cot_parts = jnp.concatenate(
        [cot_parts, jnp.broadcast_to(meta[None], (groups, tok_rows, META))], axis=2
    )
    cot_parts = lax.all_to_all(cot_parts, DP, split_axis=0, concat_axis=0, tiled=True)
    cot_pack = lax.all_gather(
        cot_parts.reshape(groups * tok_rows, share + META), "zl", axis=0, tiled=True
    )
    weights = lax.all_gather(gate_up[0], DP, axis=0, tiled=True)
    tok_pick, _ = pickers(tok_pack[:, width:], line, tok_rows, top)
    rows = jnp.dot(tok_pick, tok_pack[:, :width], preferred_element_type=jnp.float32).astype(bf16)
    rows = lax.all_to_all(
        rows.reshape(plane, line * CAP, width), PLANE, split_axis=0, concat_axis=0, tiled=True
    ).reshape(plane * line * CAP, width)
    _, cot_pick = pickers(cot_pack[:, share:], line * groups, tok_rows, top)
    scaled = jnp.dot(cot_pick, cot_pack[:, :share], preferred_element_type=jnp.float32).astype(bf16)
    scaled = lax.all_to_all(
        scaled.reshape(plane, line * groups * CAP, share),
        PLANE,
        split_axis=0,
        concat_axis=0,
        tiled=True,
    )
    scaled = scaled.reshape(plane * line, groups, CAP, share).transpose(1, 0, 2, 3)
    scaled = scaled.reshape(groups * plane * line * CAP, share)
    pre = jnp.dot(rows, weights, preferred_element_type=jnp.float32)
    hidden = (jax.nn.silu(pre[:, :hidden_units]) * pre[:, hidden_units:]).astype(bf16)
    hidden = lax.all_gather(hidden, DP, axis=0, tiled=True)
    grad = lax.dot_general(scaled, hidden, contract_rows, preferred_element_type=jnp.float32)
    correct_one = 1.0 - BETA_ONE**OPT_STEP
    correct_two = 1.0 - BETA_TWO**OPT_STEP
    first = BETA_ONE * moment1[0].astype(jnp.float32) + (1.0 - BETA_ONE) * grad
    second = BETA_TWO * moment2[0].astype(jnp.float32) + (1.0 - BETA_TWO) * grad * grad
    direction = first / correct_one / (jnp.sqrt(second / correct_two) + ADAM_EPS)
    updated = (down[0].astype(jnp.float32) - LEARN_RATE * direction).astype(bf16)
    block_cols = hidden_units // groups
    piece_rows = share // experts
    pieces = updated.reshape(experts, piece_rows, groups, block_cols).transpose(0, 2, 1, 3)
    pieces = pieces.reshape(experts * groups, piece_rows * block_cols)
    spread = lax.all_to_all(pieces, EXPERT + DP, split_axis=0, concat_axis=0, tiled=True)
    spread = spread.reshape(experts, groups * piece_rows * block_cols)
    picked = jnp.take(spread, placement, axis=0)
    landed = lax.all_to_all(picked, EXPERT, split_axis=0, concat_axis=0, tiled=True)
    landed = landed.reshape(experts, groups, piece_rows, block_cols).transpose(1, 0, 2, 3)
    return landed.reshape(1, width, block_cols)


def solution(mesh):
    grid = Mesh(mesh.devices.reshape(4, 8, 4, 2, 2), EXPERT + DP)
    every = P(EXPERT + DP, None)
    owned = P(EXPERT, DP, None)
    placed = (every, every, every, every, owned, owned, owned, owned, P())
    return jax.shard_map(
        shards, mesh=grid, in_specs=placed, out_specs=P(EXPERT, None, DP), check_vma=False
    )
```

profile of v0, /device:TPU:1, one launch (start us, length us, event | category | flops | bytes accessed | tf_op | source)
XLA Modules:
  0.0 447.6 jit_solution(951209966834745455)
XLA Ops:
  6.5 0.0 copy-start.3
  6.5 0.0 all-gather.6.cloned.1.call-start
  6.5 0.7 all-gather.6.cloned.1.call-update
  7.3 0.0 copy-done.3
  7.3 0.1 copy.84
  7.4 0.0 copy-done.2
  7.4 0.1 copy.83
  7.4 0.0 copy-done
  7.4 0.1 concatenate.12
  7.5 63.2 %all_gather.13 = bf16[128,2176]{1,0:T(8,128)(2,1)S(1)} all-gather(bf16[16,2176]{1,0:T(8,128)(2,1)S(1)} %concatenate.12), channel_id=1, replica_groups=mesh['x'=4,'zl'=8,'y'=4,'zh'=2,'core'=2] {'zl'}, dimensions={0}, use_global_device_ids=true | all-gather | bytes 626688 | tf_op jit(solution)/shard_map/all_gather | solution.py:64
  70.8 0.1 copy.99
  70.9 0.1 convert_reduce_fusion
  71.0 0.2 fusion.14
  71.2 1.6 convolution_convert_fusion
  72.8 5.8 %all-to-all-start.2 = ((bf16[16,16,2048]{2,1,0:T(8,128)(2,1)}), bf16[16,16,2048]{2,1,0:T(8,128)(2,1)S(1)}, u32[]{:S(2)}, u32[]{:S(2)}) async-start(bf16[16,16,2048]{2,1,0:T(8,128)(2,1)} %bitcast.6), calls=%async_computation.2 | async-start | bytes 2097152 | tf_op jit(solution)/shard_map/all_to_all | solution.py:76
  78.6 0.0 copy-done.1
  78.7 0.1 pad_maximum_fusion.1
  78.8 0.6 copy.85
  79.5 11.3 %all-to-all-done.2 = bf16[16,16,2048]{2,1,0:T(8,128)(2,1)S(1)} async-done(((bf16[16,16,2048]{2,1,0:T(8,128)(2,1)}), bf16[16,16,2048]{2,1,0:T(8,128)(2,1)S(1)}, u32[]{:S(2)}, u32[]{:S(2)}) %all-to-all-start.2) | async-done | bytes 1048608 | tf_op jit(solution)/shard_map/all_to_all | solution.py:76
  90.8 78.6 %all-to-all-start = ((bf16[4,16,640]{2,1,0:T(8,128)(2,1)}), bf16[4,16,640]{2,1,0:T(8,128)(2,1)S(1)}, u32[]{:S(2)}, u32[]{:S(2)}) async-start(bf16[4,16,640]{2,1,0:T(8,128)(2,1)} %copy.85), calls=%async_computation | async-start | bytes 163840 | tf_op jit(solution)/shard_map/all_to_all | solution.py:69
  169.4 0.0 all-gather.4.cloned.1.call-start
  169.4 18.9 %all-gather.6.cloned.1.call-done = bf16[1,2048,1536]{2,1,0:T(8,128)(2,1)} async-done(((bf16[1,512,1536]{2,1,0:T(8,128)(2,1)}), bf16[1,2048,1536]{2,1,0:T(8,128)(2,1)}) %all-gather.6.cloned.1.call-update) | async-done | bytes 6291472 | tf_op jit(solution)/shard_map/all_gather | solution.py:73
  188.3 4.6 %fusion = f32[256,1536]{1,0:T(8,128)S(1)} fusion(bf16[256,2048]{1,0:T(8,128)(2,1)S(1)} %bitcast.38, bf16[1,2048,1536]{2,1,0:T(8,128)(2,1)} %all-gather.6.cloned.1.call-done), kind=kOutput, calls=%fused_computation.1 | convolution fusion | flops 1610612736 | bytes 8912896 | tf_op jit(solution)/shard_map/dot_general | solution.py:90
  192.9 1.0 fusion.24
  193.8 0.0 all-gather.4.cloned.1.call-update
  193.9 0.0 all-to-all-done
  193.9 79.7 %all_gather.12 = bf16[512,640]{1,0:T(8,128)(2,1)S(1)} all-gather(bf16[64,640]{1,0:T(8,128)(2,1)S(1)} %bitcast.40), channel_id=1, replica_groups=mesh['x'=4,'zl'=8,'y'=4,'zh'=2,'core'=2] {'zl'}, dimensions={0}, use_global_device_ids=true | all-gather | bytes 737280 | tf_op jit(solution)/shard_map/all_gather | solution.py:70
  273.6 0.1 fusion.81
  273.7 0.1 copy.97
  273.8 0.1 copy.98
  273.9 0.1 fusion.32
  274.0 0.7 fusion.13
  274.7 2.0 convolution_convert_fusion.1
  276.8 20.4 %all_to_all.31 = bf16[16,64,512]{2,1,0:T(8,128)(2,1)S(1)} all-to-all(bf16[16,64,512]{2,1,0:T(8,128)(2,1)} %bitcast.39), channel_id=1, replica_groups=mesh['x'=4,'zl'=8,'y'=4,'zh'=2,'core'=2] {'x','y'}, dimensions={0} | all-to-all | bytes 2097152 | tf_op jit(solution)/shard_map/all_to_all | solution.py:81
  297.1 0.4 reshape.253
  297.6 0.7 copy.88
  298.3 0.0 copy-start.4
  298.3 0.4 reshape.254
  298.7 0.0 all-gather.4.cloned.1.call-done
  298.8 0.6 copy-done.4
  299.4 3.9 fusion.10
  303.3 0.9 reshape.257
  304.2 0.4 copy.91
  304.6 1.8 all_to_all.25
  306.4 0.5 broadcast.427
  306.9 5.4 %reduce.1 = bf16[512,768]{1,0:T(8,128)(2,1)S(1)} reduce(bf16[512,1,768]{2,1,0:T(2,128)(2,1)S(1)} %all_to_all.25, bf16[]{:T(256)} %broadcast.427), dimensions={1}, to_apply=%all_to_all.25.reduce_sub_computation | reduce | bytes 1572866 | tf_op jit(solution)/shard_map/all_to_all | solution.py:104
  312.3 0.0 copy-start.5
  312.4 1.1 reshape.273
  313.4 18.7 %all-to-all-start.3 = ((bf16[512,2,384]{2,1,0:T(2,128)(2,1)}), bf16[512,2,384]{2,1,0:T(2,128)(2,1)S(1)}, u32[]{:S(2)}, u32[]{:S(2)}) async-start(bf16[512,2,384]{2,1,0:T(2,128)(2,1)} %reshape.273), calls=%async_computation.3 | async-start | bytes 1572864 | tf_op jit(solution)/shard_map/all_to_all | solution.py:104
  332.2 0.0 copy-done.5
  332.2 46.2 %all-to-all-done.3 = bf16[512,2,384]{2,1,0:T(2,128)(2,1)S(1)} async-done(((bf16[512,2,384]{2,1,0:T(2,128)(2,1)}), bf16[512,2,384]{2,1,0:T(2,128)(2,1)S(1)}, u32[]{:S(2)}, u32[]{:S(2)}) %all-to-all-start.3) | async-done | bytes 786464 | tf_op jit(solution)/shard_map/all_to_all | solution.py:104
  378.4 0.6 reshape.274
  379.1 5.0 %reduce = bf16[512,768]{1,0:T(8,128)(2,1)S(1)} reduce(bf16[512,1,768]{2,1,0:T(2,128)(2,1)S(1)} %reshape.274, bf16[]{:T(256)} %constant.215), dimensions={1}, to_apply=%all_to_all.23.reduce_sub_computation | reduce | bytes 1572866 | tf_op jit(solution)/shard_map/all_to_all | solution.py:104
  384.1 0.5 reshape.258
  384.5 1.0 gather_fusion
  385.6 0.1 bitcast_select_fusion
  385.7 1.2 reduce.2
  386.9 0.6 reshape.275
  387.5 48.3 %all_to_all.32 = bf16[128,2,1536]{2,1,0:T(2,128)(2,1)S(1)} all-to-all(bf16[128,2,1536]{2,1,0:T(2,128)(2,1)S(1)} %reshape.275), channel_id=1, replica_groups=mesh['x'=4,'zl'=8,'y'=4,'zh'=2,'core'=2] {'x','zl','y'}, dimensions={0} | all-to-all | bytes 1572864 | tf_op jit(solution)/shard_map/all_to_all | solution.py:107
  435.7 0.6 reshape.276
  436.4 1.8 copy.94
  438.1 0.7 copy.95
  438.9 0.7 reshape.260
  439.5 1.2 copy.96
  (22 shorter events, 0.2 us)
Async XLA Ops:
  6.5 0.7 copy-start.3
  6.5 0.8 copy-start.2
  6.5 0.9 copy-start
  6.5 181.8 %all-gather.6.cloned.1.call-start = ((), (), s32[]{:S(2)}) async-start(), calls=%async_computation.6 | async-start | bytes 7864320 | tf_op jit(solution)/shard_map/all_gather | solution.py:73
  71.2 7.5 %copy-start.1 = (bf16[16,2048]{1,0:T(8,128)(2,1)S(1)}, bf16[16,2048]{1,0:T(8,128)(2,1)}, u32[]{:S(2)}) copy-start(bf16[16,2048]{1,0:T(8,128)(2,1)} %param.10) | copy-start | bytes 196612
  72.8 18.0 %all-to-all-start.2 = ((bf16[16,16,2048]{2,1,0:T(8,128)(2,1)}), bf16[16,16,2048]{2,1,0:T(8,128)(2,1)S(1)}, u32[]{:S(2)}, u32[]{:S(2)}) async-start(bf16[16,16,2048]{2,1,0:T(8,128)(2,1)} %bitcast.6), calls=%async_computation.2 | async-start | bytes 2097152 | tf_op jit(solution)/shard_map/all_to_all | solution.py:76
  90.8 103.1 %all-to-all-start = ((bf16[4,16,640]{2,1,0:T(8,128)(2,1)}), bf16[4,16,640]{2,1,0:T(8,128)(2,1)S(1)}, u32[]{:S(2)}, u32[]{:S(2)}) async-start(bf16[4,16,640]{2,1,0:T(8,128)(2,1)} %copy.85), calls=%async_computation | async-start | bytes 163840 | tf_op jit(solution)/shard_map/all_to_all | solution.py:69
  169.4 129.4 %all-gather.4.cloned.1.call-start = ((), (), s32[]{:S(2)}) async-start(), calls=%async_computation.5 | async-start | bytes 1966080 | tf_op jit(solution)/shard_map/all_gather | solution.py:92
  298.3 1.1 copy-start.4
  312.3 19.8 %copy-start.5 = (s32[128]{0:T(128)S(1)}, s32[128]{0:T(128)}, u32[]{:S(2)}) copy-start(s32[128]{0:T(128)} %param.17) | copy-start | bytes 1540
  313.4 65.0 %all-to-all-start.3 = ((bf16[512,2,384]{2,1,0:T(2,128)(2,1)}), bf16[512,2,384]{2,1,0:T(2,128)(2,1)S(1)}, u32[]{:S(2)}, u32[]{:S(2)}) async-start(bf16[512,2,384]{2,1,0:T(2,128)(2,1)} %reshape.273), calls=%async_computation.3 | async-start | bytes 1572864 | tf_op jit(solution)/shard_map/all_to_all | solution.py:104
Sparse Core Ops, SparseCore 0:
  9.4 178.8 all-gather.5
  194.0 86.3 all-gather.3
where the time goes:
time: 448 us
  blocking collectives  212 us (47%)
  starting transfers between devices  103 us (23%)
  waiting for transfers between devices  77.2 us (17%)
  local copies, waits for them, and re-layouts  15.9 us (4%)
  between operations  13.7 us (3%)
  other arithmetic  13.1 us (3%)
  matrix products  13 us (3%)
    all_gather x1, blocking collectives, shards(): lax.all_gather(cot_parts.reshape(groups * tok_rows, share + META), 'zl',...  79.7 us
    all_to_all x1, starting transfers between devices, shards(): lax.all_to_all(cot_parts, DP, split_axis=0, concat_axis=0, tiled=True)  78.6 us
    all_gather x1, blocking collectives, shards(): lax.all_gather(jnp.concatenate([tokens, meta], axis=1), 'zl', axis=0, til...  63.2 us
    all_to_all x1, blocking collectives, shards(): lax.all_to_all(picked, EXPERT, split_axis=0, concat_axis=0, tiled=True)  48.3 us
    all_to_all x1, waiting for transfers between devices, shards(): lax.all_to_all(pieces, EXPERT + DP, split_axis=0, concat_axis=0, tiled=True)  46.2 us
    all_to_all x1, blocking collectives, shards(): lax.all_to_all(scaled.reshape(plane, line * groups * CAP, share), PLANE,...  20.4 us
    all_gather x1, waiting for transfers between devices, shards(): weights = lax.all_gather(gate_up[0], DP, axis=0, tiled=True)  18.9 us
    all_to_all x1, starting transfers between devices, shards(): lax.all_to_all(pieces, EXPERT + DP, split_axis=0, concat_axis=0, tiled=True)  18.7 us
  transfers between devices with their start and end apart: 5, of which 3 were waited for; matrix products, arithmetic and copies ran while one was open for 3% of the time, Pallas kernels for 0%

commit v1 on v0

--- a/solution.py
+++ b/solution.py
@@ -1,3 +1,4 @@
+import functools
 import jax
 import jax.numpy as jnp
 from jax import lax
@@ -14,6 +15,16 @@
 CAP = 2
 META = 128
 contract_rows = (((0,), (0,)), ((), ()))
+
+
+def attach_local_data_on(w_in, mesh_ax):
+    k_now = jnp.concatenate(
+        lax.all_to_all(jnp.stack(lax.axis_size(mesh_ax) * [w_in], 0), mesh_ax, 0, 0), 0
+    )
+    return k_now
+
+
+group_the_spot = functools.partial(attach_local_data_on, mesh_ax="zl")
 
 
 def pickers(meta, blocks, block_rows, top):
@@ -67,9 +78,7 @@
         [cot_parts, jnp.broadcast_to(meta[None], (groups, tok_rows, META))], axis=2
     )
     cot_parts = lax.all_to_all(cot_parts, DP, split_axis=0, concat_axis=0, tiled=True)
-    cot_pack = lax.all_gather(
-        cot_parts.reshape(groups * tok_rows, share + META), "zl", axis=0, tiled=True
-    )
+    cot_pack = group_the_spot(cot_parts.reshape(groups * tok_rows, share + META))
     weights = lax.all_gather(gate_up[0], DP, axis=0, tiled=True)
     tok_pick, _ = pickers(tok_pack[:, width:], line, tok_rows, top)
     rows = jnp.dot(tok_pick, tok_pack[:, :width], preferred_element_type=jnp.float32).astype(bf16)

time: 448 us -> 412 us (0.920)
  blocking collectives: 212 us -> 156 us
  waiting for transfers between devices: 77.2 us -> 116 us
  starting transfers between devices: 103 us -> 83.9 us
    all_gather x1 -> x0, blocking collectives: 79.7 us -> none  [shards(): lax.all_gather(cot_parts.reshape(groups * tok_rows, share + META), 'zl',...]
    all_to_all x1, starting transfers between devices: 78.6 us -> 16.6 us  [shards(): lax.all_to_all(cot_parts, DP, split_axis=0, concat_axis=0, tiled=True)]
    all_to_all x1, starting transfers between devices: 5.83 us -> 56.8 us  [attach_local_data_on(): lax.all_to_all(jnp.stack(lax.axis_size(mesh_ax) * [w_in], 0), mesh_ax, 0, 0)]
    all_gather x1, waiting for transfers between devices: 0.02 us -> 48.6 us  [shards(): hidden = lax.all_gather(hidden, DP, axis=0, tiled=True)]
    all_to_all x0 -> x1, blocking collectives: none -> 22.8 us  [shards(): lax.all_to_all(rows.reshape(plane, line * CAP, width), PLANE, split_axis=...]
    all_to_all x1, waiting for transfers between devices: 11.3 us -> 2.35 us  [attach_local_data_on(): lax.all_to_all(jnp.stack(lax.axis_size(mesh_ax) * [w_in], 0), mesh_ax, 0, 0)]
    all_to_all x1, starting transfers between devices: 18.7 us -> 10.5 us  [shards(): lax.all_to_all(pieces, EXPERT + DP, split_axis=0, concat_axis=0, tiled=True)]
  transfers between devices with their start and end apart: 5 -> 5, of which waited for: 3 -> 4; matrix products, arithmetic and copies ran while one was open for 3% -> 3% of each run, Pallas kernels for 0% -> 0%
where the time goes in v1:
time: 412 us; the launch traced here: 411 us
  blocking collectives  156 us (38%)
  waiting for transfers between devices  116 us (28%)
  starting transfers between devices  83.9 us (20%)
  local copies, waits for them, and re-layouts  16.1 us (4%)
  between operations  13.7 us (3%)
  other arithmetic  13.1 us (3%)
  matrix products  12 us (3%)
    all_gather x1, blocking collectives, shards(): lax.all_gather(jnp.concatenate([tokens, meta], axis=1), 'zl', axis=0, til...  67 us
    all_to_all x1, starting transfers between devices, attach_local_data_on(): lax.all_to_all(jnp.stack(lax.axis_size(mesh_ax) * [w_in], 0), mesh_ax, 0, 0)  56.8 us
    all_gather x1, waiting for transfers between devices, shards(): hidden = lax.all_gather(hidden, DP, axis=0, tiled=True)  48.6 us
    all_to_all x1, blocking collectives, shards(): lax.all_to_all(picked, EXPERT, split_axis=0, concat_axis=0, tiled=True)  48.3 us
    all_to_all x1, waiting for transfers between devices, shards(): lax.all_to_all(pieces, EXPERT + DP, split_axis=0, concat_axis=0, tiled=True)  46.2 us
    all_to_all x1, blocking collectives, shards(): lax.all_to_all(rows.reshape(plane, line * CAP, width), PLANE, split_axis=...  22.8 us
    all_to_all x1, blocking collectives, shards(): lax.all_to_all(scaled.reshape(plane, line * groups * CAP, share), PLANE,...  18.1 us
    all_gather x1, waiting for transfers between devices, shards(): weights = lax.all_gather(gate_up[0], DP, axis=0, tiled=True)  18 us
  transfers between devices with their start and end apart: 5, of which 4 were waited for; matrix products, arithmetic and copies ran while one was open for 3% of the time, Pallas kernels for 0%

profile of v1, /device:TPU:1, one launch (start us, length us, event | category | flops | bytes accessed | tf_op | source)
XLA Modules:
  0.0 411.0 jit_solution(6388951015111669551)
XLA Ops:
  6.5 0.0 all-gather.6.cloned.1.call-start
  6.6 0.7 all-gather.6.cloned.1.call-update
  7.3 0.0 copy-done.3
  7.3 0.1 copy.99
  7.4 0.0 copy-done.2
  7.4 0.1 copy.98
  7.4 0.0 copy-done
  7.5 0.1 pad_maximum_fusion.1
  7.6 0.6 copy.100
  8.3 16.6 %all-to-all-start = ((bf16[4,16,640]{2,1,0:T(8,128)(2,1)}), bf16[4,16,640]{2,1,0:T(8,128)(2,1)S(1)}, u32[]{:S(2)}, u32[]{:S(2)}) async-start(bf16[4,16,640]{2,1,0:T(8,128)(2,1)} %copy.100), calls=%async_computation | async-start | bytes 163840 | tf_op jit(solution)/shard_map/all_to_all | solution.py:80
  24.9 0.0 copy-done.1
  24.9 0.1 concatenate.12
  25.0 67.0 %all_gather.9 = bf16[128,2176]{1,0:T(8,128)(2,1)S(1)} all-gather(bf16[16,2176]{1,0:T(8,128)(2,1)S(1)} %concatenate.12), channel_id=1, replica_groups=mesh['x'=4,'zl'=8,'y'=4,'zh'=2,'core'=2] {'zl'}, dimensions={0}, use_global_device_ids=true | all-gather | bytes 626688 | tf_op jit(solution)/shard_map/all_gather | solution.py:75
  92.0 0.1 copy.114
  92.1 0.1 convert_reduce_fusion
  92.2 0.2 fusion.14
  92.4 0.6 convolution_convert_fusion
  93.0 0.0 all-to-all-done
  93.0 22.8 %all_to_all.36 = bf16[16,16,2048]{2,1,0:T(8,128)(2,1)S(1)} all-to-all(bf16[16,16,2048]{2,1,0:T(8,128)(2,1)S(1)} %bitcast.37), channel_id=1, replica_groups=mesh['x'=4,'zl'=8,'y'=4,'zh'=2,'core'=2] {'x','y'}, dimensions={0} | all-to-all | bytes 2097152 | tf_op jit(solution)/shard_map/all_to_all | solution.py:85
  115.9 0.9 stack.3
  116.7 56.8 %all-to-all-start.1 = ((bf16[8,64,640]{2,1,0:T(8,128)(2,1)}), bf16[8,64,640]{2,1,0:T(8,128)(2,1)S(1)}, u32[]{:S(2)}, u32[]{:S(2)}) async-start(bf16[8,64,640]{2,1,0:T(8,128)(2,1)} %stack.3), calls=%async_computation.1 | async-start | bytes 1310720 | tf_op jit(solution)/shard_map/all_to_all | solution.py:22
  173.6 0.0 all-gather.4.cloned.1.call-start
  173.6 18.0 %all-gather.6.cloned.1.call-done = bf16[1,2048,1536]{2,1,0:T(8,128)(2,1)} async-done(((bf16[1,512,1536]{2,1,0:T(8,128)(2,1)}), bf16[1,2048,1536]{2,1,0:T(8,128)(2,1)}) %all-gather.6.cloned.1.call-update) | async-done | bytes 6291472 | tf_op jit(solution)/shard_map/all_gather | solution.py:82
  191.6 4.6 %fusion = f32[256,1536]{1,0:T(8,128)S(1)} fusion(bf16[256,2048]{1,0:T(8,128)(2,1)S(1)} %bitcast.42, bf16[1,2048,1536]{2,1,0:T(8,128)(2,1)} %all-gather.6.cloned.1.call-done), kind=kOutput, calls=%fused_computation.1 | convolution fusion | flops 1610612736 | bytes 8912896 | tf_op jit(solution)/shard_map/dot_general | solution.py:99
  196.1 1.0 fusion.24
  197.2 0.0 all-gather.4.cloned.1.call-update
  197.2 2.4 all-to-all-done.1
  199.6 0.1 fusion.81
  199.7 0.1 copy.112
  199.8 0.1 copy.113
  199.8 0.1 fusion.32
  200.0 0.7 fusion.13
  200.7 2.0 convolution_convert_fusion.1
  202.7 18.1 %all_to_all.37 = bf16[16,64,512]{2,1,0:T(8,128)(2,1)S(1)} all-to-all(bf16[16,64,512]{2,1,0:T(8,128)(2,1)} %bitcast.43), channel_id=1, replica_groups=mesh['x'=4,'zl'=8,'y'=4,'zh'=2,'core'=2] {'x','y'}, dimensions={0} | all-to-all | bytes 2097152 | tf_op jit(solution)/shard_map/all_to_all | solution.py:90
  220.8 0.4 reshape.255
  221.3 0.7 copy.103
  222.0 0.0 copy-start.4
  222.0 0.4 reshape.256
  222.5 48.6 %all-gather.4.cloned.1.call-done = bf16[1024,768]{1,0:T(8,128)(2,1)} async-done(((bf16[256,768]{1,0:T(8,128)(2,1)}), bf16[1024,768]{1,0:T(8,128)(2,1)}) %all-gather.4.cloned.1.call-update) | async-done | bytes 1572880 | tf_op jit(solution)/shard_map/all_gather | solution.py:101
  271.1 0.0 copy-done.4
  271.1 3.9 fusion.10
  275.0 0.9 reshape.259
  275.9 0.4 copy.106
  276.3 1.8 all_to_all.29
  278.1 0.5 broadcast.428
  278.6 5.4 %reduce.1 = bf16[512,768]{1,0:T(8,128)(2,1)S(1)} reduce(bf16[512,1,768]{2,1,0:T(2,128)(2,1)S(1)} %all_to_all.29, bf16[]{:T(256)} %broadcast.428), dimensions={1}, to_apply=%all_to_all.29.reduce_sub_computation | reduce | bytes 1572866 | tf_op jit(solution)/shard_map/all_to_all | solution.py:113
  284.0 0.0 copy-start.5
  284.0 1.1 reshape.275
  285.1 10.5 %all-to-all-start.4 = ((bf16[512,2,384]{2,1,0:T(2,128)(2,1)}), bf16[512,2,384]{2,1,0:T(2,128)(2,1)S(1)}, u32[]{:S(2)}, u32[]{:S(2)}) async-start(bf16[512,2,384]{2,1,0:T(2,128)(2,1)} %reshape.275), calls=%async_computation.4 | async-start | bytes 1572864 | tf_op jit(solution)/shard_map/all_to_all | solution.py:113
  295.6 0.0 copy-done.5
  295.6 46.2 %all-to-all-done.4 = bf16[512,2,384]{2,1,0:T(2,128)(2,1)S(1)} async-done(((bf16[512,2,384]{2,1,0:T(2,128)(2,1)}), bf16[512,2,384]{2,1,0:T(2,128)(2,1)S(1)}, u32[]{:S(2)}, u32[]{:S(2)}) %all-to-all-start.4) | async-done | bytes 786464 | tf_op jit(solution)/shard_map/all_to_all | solution.py:113
  341.9 0.6 reshape.276
  342.5 5.0 %reduce = bf16[512,768]{1,0:T(8,128)(2,1)S(1)} reduce(bf16[512,1,768]{2,1,0:T(2,128)(2,1)S(1)} %reshape.276, bf16[]{:T(256)} %constant.215), dimensions={1}, to_apply=%all_to_all.27.reduce_sub_computation | reduce | bytes 1572866 | tf_op jit(solution)/shard_map/all_to_all | solution.py:113
  347.5 0.5 reshape.260
  348.0 1.0 gather_fusion
  349.0 0.1 bitcast_select_fusion
  349.1 1.2 reduce.2
  350.3 0.6 reshape.277
  350.9 48.3 %all_to_all.38 = bf16[128,2,1536]{2,1,0:T(2,128)(2,1)S(1)} all-to-all(bf16[128,2,1536]{2,1,0:T(2,128)(2,1)S(1)} %reshape.277), channel_id=1, replica_groups=mesh['x'=4,'zl'=8,'y'=4,'zh'=2,'core'=2] {'x','zl','y'}, dimensions={0} | all-to-all | bytes 1572864 | tf_op jit(solution)/shard_map/all_to_all | solution.py:116
  399.1 0.6 reshape.278
  399.8 1.8 copy.109
  401.6 0.7 copy.110
  402.3 0.7 reshape.262
  403.0 1.2 copy.111
  (23 shorter events, 0.2 us)
Async XLA Ops:
  6.5 0.7 copy-start.3
  6.5 0.8 copy-start.2
  6.5 0.9 copy-start
  6.5 18.3 %copy-start.1 = (bf16[16,2048]{1,0:T(8,128)(2,1)S(1)}, bf16[16,2048]{1,0:T(8,128)(2,1)}, u32[]{:S(2)}) copy-start(bf16[16,2048]{1,0:T(8,128)(2,1)} %param.9) | copy-start | bytes 196612
  6.5 185.0 %all-gather.6.cloned.1.call-start = ((), (), s32[]{:S(2)}) async-start(), calls=%async_computation.7 | async-start | bytes 7864320 | tf_op jit(solution)/shard_map/all_gather | solution.py:82
  8.3 84.7 %all-to-all-start = ((bf16[4,16,640]{2,1,0:T(8,128)(2,1)}), bf16[4,16,640]{2,1,0:T(8,128)(2,1)S(1)}, u32[]{:S(2)}, u32[]{:S(2)}) async-start(bf16[4,16,640]{2,1,0:T(8,128)(2,1)} %copy.100), calls=%async_computation | async-start | bytes 163840 | tf_op jit(solution)/shard_map/all_to_all | solution.py:80
  116.7 82.8 %all-to-all-start.1 = ((bf16[8,64,640]{2,1,0:T(8,128)(2,1)}), bf16[8,64,640]{2,1,0:T(8,128)(2,1)S(1)}, u32[]{:S(2)}, u32[]{:S(2)}) async-start(bf16[8,64,640]{2,1,0:T(8,128)(2,1)} %stack.3), calls=%async_computation.1 | async-start | bytes 1310720 | tf_op jit(solution)/shard_map/all_to_all | solution.py:22
  173.6 97.5 %all-gather.4.cloned.1.call-start = ((), (), s32[]{:S(2)}) async-start(), calls=%async_computation.6 | async-start | bytes 1966080 | tf_op jit(solution)/shard_map/all_gather | solution.py:101
  222.0 49.1 %copy-start.4 = (bf16[1,512,768]{2,1,0:T(8,128)(2,1)S(1)}, bf16[1,512,768]{2,1,0:T(8,128)(2,1)}, u32[]{:S(2)}) copy-start(bf16[1,512,768]{2,1,0:T(8,128)(2,1)} %param.16) | copy-start | bytes 2359300
  284.0 11.6 %copy-start.5 = (s32[128]{0:T(128)S(1)}, s32[128]{0:T(128)}, u32[]{:S(2)}) copy-start(s32[128]{0:T(128)} %param.17) | copy-start | bytes 1540
  285.1 56.8 %all-to-all-start.4 = ((bf16[512,2,384]{2,1,0:T(2,128)(2,1)}), bf16[512,2,384]{2,1,0:T(2,128)(2,1)S(1)}, u32[]{:S(2)}, u32[]{:S(2)}) async-start(bf16[512,2,384]{2,1,0:T(2,128)(2,1)} %reshape.275), calls=%async_computation.4 | async-start | bytes 1572864 | tf_op jit(solution)/shard_map/all_to_all | solution.py:113
Sparse Core Ops, SparseCore 0:
  9.5 182.0 all-gather.5
  197.3 73.7 all-gather.3
